TPU v7x, 256 devices: a whole 4x4x8 slice. The times are simulated.
256 devices in a mesh: row: 16 (over x_hi, y, core), col: 16 (over x_lo, z).
Axes of the slice: x: 4 (x_hi: 2, x_lo: 2; x = x_hi * 2 + x_lo), y: 4, z: 8, core: 2. Of those that a mesh axis runs over, the one named last changes fastest.
Arguments:
- points: bfloat16 [16, 131072], P(None, ('row', 'col')), may hold values from -6 to 6
- spread: bfloat16 [131072], P(('row', 'col')), may hold values from 2 to 12
- vectors: bfloat16 [8, 131072], P(None, ('row', 'col')), may hold values from -6 to 6
Outputs:
- basis: float32 [8, 131072], P(None, ('row', 'col'))
All inputs are finite; a program needn't handle non-finite values.
Results may differ from a plain program's by a relative error of at most 0.012.
Values may be sent and summed in bfloat16 or wider, within the bound.
A program may use at most 64 MiB of HBM per device.

v0:
```python
import math

import jax
import jax.numpy as jnp
from jax import lax
from jax.sharding import PartitionSpec as P


def squared_norm(pts):
    values = pts.astype(jnp.float32)
    return jnp.sum(values * values, axis=0)


def affinity_block(pts_left, norm_left, scale_left, pts_right, norm_right, scale_right):
    cross = lax.dot_general(
        pts_left, pts_right, (((0,), (0,)), ((), ())), preferred_element_type=jnp.float32
    )
    dist = norm_left[:, None] + norm_right[None, :] - 2.0 * cross
    denom = scale_left.astype(jnp.float32)[:, None] * scale_right.astype(jnp.float32)[None, :]
    return jnp.exp(-dist / denom).astype(jnp.bfloat16)


def with_ones(vecs):
    return jnp.concatenate([vecs, jnp.ones((1,) + vecs.shape[1:], jnp.bfloat16)], axis=0)


def shards(points, spread, vectors):
    n_row = lax.axis_size("row")
    n_col = lax.axis_size("col")
    local = points.shape[1]
    dims = points.shape[0]
    kvec = vectors.shape[0]
    col_pts, col_scale, col_vecs = (
        lax.all_gather(points, "row", axis=1, tiled=True),
        lax.all_gather(spread, "row", axis=0, tiled=True),
        lax.all_gather(vectors, "row", axis=1, tiled=True),
    )
    col_ext = with_ones(col_vecs)
    col_norm = squared_norm(col_pts)
    row_pts, row_scale = (
        lax.all_gather(points, "col", axis=1, tiled=True),
        lax.all_gather(spread, "col", axis=0, tiled=True),
    )
    row_norm = squared_norm(row_pts)
    group = math.gcd(n_col, max(1, 512 // local))
    size = group * local
    nblocks = n_col // group
    pts_blocks = jnp.transpose(row_pts.reshape(dims, nblocks, size), (1, 0, 2))
    norm_blocks = row_norm.reshape(nblocks, size)
    scale_blocks = row_scale.reshape(nblocks, size)

    def one_block(operands):
        pts_blk, norm_blk, scale_blk = operands
        affinity = affinity_block(pts_blk, norm_blk, scale_blk, col_pts, col_norm, col_scale)
        return lax.dot_general(
            col_ext, affinity, (((1,), (1,)), ((), ())), preferred_element_type=jnp.float32
        )

    parts = lax.map(one_block, (pts_blocks, norm_blocks, scale_blocks))
    row_part = jnp.transpose(parts, (1, 0, 2)).reshape(kvec + 1, n_col * local)
    total = lax.psum_scatter(row_part, "col", scatter_dimension=1, tiled=True)
    update = total[:kvec] / total[kvec : kvec + 1]
    gram_local = jnp.sum(update[:, None, :] * update[None, :, :], axis=2)
    gram = lax.psum(gram_local, ("row", "col"))
    lower = jnp.linalg.cholesky(gram)
    solved = lax.linalg.triangular_solve(lower, update, left_side=True, lower=True)
    count = local * n_row * n_col
    return jnp.sqrt(jnp.float32(count)) * solved


def solution(mesh):
    in_specs = (P(None, ("row", "col")), P(("row", "col")), P(None, ("row", "col")))
    out_specs = P(None, ("row", "col"))
    return jax.shard_map(shards, mesh=mesh, in_specs=in_specs, out_specs=out_specs, check_vma=False)
```

profile of v0, /device:TPU:1, one launch (start us, length us, event | category | flops | bytes accessed | tf_op | source)
XLA Modules:
  0.0 400.6 jit_solution(6532112069739902506)
XLA Ops:
  6.5 0.0 copy-start.1
  6.5 0.0 reduce-scatter.2.cloned.1.call-start
  6.5 31.7 %all_gather.15 = bf16[16,8192]{1,0:T(8,128)(2,1)S(1)} all-gather(bf16[16,512]{1,0:T(8,128)(2,1)} %param.5), channel_id=1, replica_groups=mesh['row'=16,'col'=16] {'col'}, dimensions={1}, use_global_device_ids=true | all-gather | bytes 278528 | tf_op jit(solution)/shard_map/all_gather | solution.py:41
  38.2 32.8 %all_gather.16 = bf16[16,8192]{1,0:T(8,128)(2,1)S(1)} all-gather(bf16[16,512]{1,0:T(8,128)(2,1)} %param.5), channel_id=1, replica_groups=mesh['row'=16,'col'=16] {'row'}, dimensions={1}, use_global_device_ids=true | all-gather | bytes 278528 | tf_op jit(solution)/shard_map/all_gather | solution.py:34
  71.0 0.0 copy-done.1
  71.0 19.3 %all-gather.1 = bf16[16,1,512]{2,1,0:T(2,128)(2,1)S(1)} all-gather(bf16[1,1,512]{2,1,0:T(2,128)(2,1)S(1)} %reshape.41), channel_id=1, replica_groups=mesh['row'=16,'col'=16] {'row'}, dimensions={0}, use_global_device_ids=true | all-gather | bytes 17408 | tf_op jit(solution)/shard_map/all_gather | solution.py:35
  90.3 22.7 %all-gather = bf16[16,1,512]{2,1,0:T(2,128)(2,1)S(1)} all-gather(bf16[1,1,512]{2,1,0:T(2,128)(2,1)S(1)} %reshape.41), channel_id=1, replica_groups=mesh['row'=16,'col'=16] {'col'}, dimensions={0}, use_global_device_ids=true | all-gather | bytes 17408 | tf_op jit(solution)/shard_map/all_gather | solution.py:42
  113.0 0.1 multiply_reduce_fusion.1
  113.1 0.1 copy.24
  113.2 0.0 copy-start
  113.2 0.2 copy.18
  113.4 0.1 multiply_reduce_fusion
  113.5 0.1 reduce.6
  113.6 0.3 copy-done
  113.9 27.9 %all_gather.19 = bf16[8,8192]{1,0:T(8,128)(2,1)S(1)} all-gather(bf16[8,512]{1,0:T(8,128)(2,1)S(1)} %copy-done), channel_id=1, replica_groups=mesh['row'=16,'col'=16] {'row'}, dimensions={1}, use_global_device_ids=true | all-gather | bytes 139264 | tf_op jit(solution)/shard_map/all_gather | solution.py:36
  141.8 108.7 %while.10 = (s32[]{:T(128)}, f32[16,9,512]{2,1,0:T(8,128)S(1)}, f32[16,512]{1,0:T(8,128)S(1)}, f32[8192]{0:T(1024)S(1)}, bf16[16,16,512]{2,1,0:T(8,128)(2,1)S(1)...) while((s32[]{:T(128)}, f32[16,9,512]{2,1,0:T(8,128)S(1)}, ...), condition=%wide.region_3.4_spmd, body=%wide.region_2.3_spmd.sunk | while | flops 239084032 | bytes 700525 | solution.py:59
  141.9 6.7 %fusion.23 = f32[16,9,512]{2,1,0:T(8,128)S(1)} fusion(f32[16,9,512]{2,1,0:T(8,128)S(1)} %get-tuple-element.173, s32[]{:T(128)} %get-tuple-element.172, bf16[9,8192]{1,0:T(8,128)(2,1)S(1)} %get-tuple-element.190, bf16[16,8192]{1,0:T(8,128)(2,1)S(1)} %get-tuple-element.187, f32[8192]{0:T(1024)S(1)} %convert_element_type.44, f32[512]{0:T(512)S(1)} %bitcast.58, ...), kind=kOutput, calls=%fused_computation.3.clone.1 | convolution fusion | flops 239075328 | bytes 644096 | tf_op jit(solution)/shard_map/while/body/eval_jaxpr/dot_general | solution.py:55
  148.7 6.7 %fusion.23 = f32[16,9,512]{2,1,0:T(8,128)S(1)} fusion(f32[16,9,512]{2,1,0:T(8,128)S(1)} %get-tuple-element.173, s32[]{:T(128)} %get-tuple-element.172, bf16[9,8192]{1,0:T(8,128)(2,1)S(1)} %get-tuple-element.190, bf16[16,8192]{1,0:T(8,128)(2,1)S(1)} %get-tuple-element.187, f32[8192]{0:T(1024)S(1)} %convert_element_type.44, f32[512]{0:T(512)S(1)} %bitcast.58, ...), kind=kOutput, calls=%fused_computation.3.clone.1 | convolution fusion | flops 239075328 | bytes 644096 | tf_op jit(solution)/shard_map/while/body/eval_jaxpr/dot_general | solution.py:55
  155.5 6.7 %fusion.23 = f32[16,9,512]{2,1,0:T(8,128)S(1)} fusion(f32[16,9,512]{2,1,0:T(8,128)S(1)} %get-tuple-element.173, s32[]{:T(128)} %get-tuple-element.172, bf16[9,8192]{1,0:T(8,128)(2,1)S(1)} %get-tuple-element.190, bf16[16,8192]{1,0:T(8,128)(2,1)S(1)} %get-tuple-element.187, f32[8192]{0:T(1024)S(1)} %convert_element_type.44, f32[512]{0:T(512)S(1)} %bitcast.58, ...), kind=kOutput, calls=%fused_computation.3.clone.1 | convolution fusion | flops 239075328 | bytes 644096 | tf_op jit(solution)/shard_map/while/body/eval_jaxpr/dot_general | solution.py:55
  162.3 6.7 %fusion.23 = f32[16,9,512]{2,1,0:T(8,128)S(1)} fusion(f32[16,9,512]{2,1,0:T(8,128)S(1)} %get-tuple-element.173, s32[]{:T(128)} %get-tuple-element.172, bf16[9,8192]{1,0:T(8,128)(2,1)S(1)} %get-tuple-element.190, bf16[16,8192]{1,0:T(8,128)(2,1)S(1)} %get-tuple-element.187, f32[8192]{0:T(1024)S(1)} %convert_element_type.44, f32[512]{0:T(512)S(1)} %bitcast.58, ...), kind=kOutput, calls=%fused_computation.3.clone.1 | convolution fusion | flops 239075328 | bytes 644096 | tf_op jit(solution)/shard_map/while/body/eval_jaxpr/dot_general | solution.py:55
  169.1 6.7 %fusion.23 = f32[16,9,512]{2,1,0:T(8,128)S(1)} fusion(f32[16,9,512]{2,1,0:T(8,128)S(1)} %get-tuple-element.173, s32[]{:T(128)} %get-tuple-element.172, bf16[9,8192]{1,0:T(8,128)(2,1)S(1)} %get-tuple-element.190, bf16[16,8192]{1,0:T(8,128)(2,1)S(1)} %get-tuple-element.187, f32[8192]{0:T(1024)S(1)} %convert_element_type.44, f32[512]{0:T(512)S(1)} %bitcast.58, ...), kind=kOutput, calls=%fused_computation.3.clone.1 | convolution fusion | flops 239075328 | bytes 644096 | tf_op jit(solution)/shard_map/while/body/eval_jaxpr/dot_general | solution.py:55
  175.9 6.7 %fusion.23 = f32[16,9,512]{2,1,0:T(8,128)S(1)} fusion(f32[16,9,512]{2,1,0:T(8,128)S(1)} %get-tuple-element.173, s32[]{:T(128)} %get-tuple-element.172, bf16[9,8192]{1,0:T(8,128)(2,1)S(1)} %get-tuple-element.190, bf16[16,8192]{1,0:T(8,128)(2,1)S(1)} %get-tuple-element.187, f32[8192]{0:T(1024)S(1)} %convert_element_type.44, f32[512]{0:T(512)S(1)} %bitcast.58, ...), kind=kOutput, calls=%fused_computation.3.clone.1 | convolution fusion | flops 239075328 | bytes 644096 | tf_op jit(solution)/shard_map/while/body/eval_jaxpr/dot_general | solution.py:55
  182.7 6.7 %fusion.23 = f32[16,9,512]{2,1,0:T(8,128)S(1)} fusion(f32[16,9,512]{2,1,0:T(8,128)S(1)} %get-tuple-element.173, s32[]{:T(128)} %get-tuple-element.172, bf16[9,8192]{1,0:T(8,128)(2,1)S(1)} %get-tuple-element.190, bf16[16,8192]{1,0:T(8,128)(2,1)S(1)} %get-tuple-element.187, f32[8192]{0:T(1024)S(1)} %convert_element_type.44, f32[512]{0:T(512)S(1)} %bitcast.58, ...), kind=kOutput, calls=%fused_computation.3.clone.1 | convolution fusion | flops 239075328 | bytes 644096 | tf_op jit(solution)/shard_map/while/body/eval_jaxpr/dot_general | solution.py:55
  189.5 6.7 %fusion.23 = f32[16,9,512]{2,1,0:T(8,128)S(1)} fusion(f32[16,9,512]{2,1,0:T(8,128)S(1)} %get-tuple-element.173, s32[]{:T(128)} %get-tuple-element.172, bf16[9,8192]{1,0:T(8,128)(2,1)S(1)} %get-tuple-element.190, bf16[16,8192]{1,0:T(8,128)(2,1)S(1)} %get-tuple-element.187, f32[8192]{0:T(1024)S(1)} %convert_element_type.44, f32[512]{0:T(512)S(1)} %bitcast.58, ...), kind=kOutput, calls=%fused_computation.3.clone.1 | convolution fusion | flops 239075328 | bytes 644096 | tf_op jit(solution)/shard_map/while/body/eval_jaxpr/dot_general | solution.py:55
  196.3 6.7 %fusion.23 = f32[16,9,512]{2,1,0:T(8,128)S(1)} fusion(f32[16,9,512]{2,1,0:T(8,128)S(1)} %get-tuple-element.173, s32[]{:T(128)} %get-tuple-element.172, bf16[9,8192]{1,0:T(8,128)(2,1)S(1)} %get-tuple-element.190, bf16[16,8192]{1,0:T(8,128)(2,1)S(1)} %get-tuple-element.187, f32[8192]{0:T(1024)S(1)} %convert_element_type.44, f32[512]{0:T(512)S(1)} %bitcast.58, ...), kind=kOutput, calls=%fused_computation.3.clone.1 | convolution fusion | flops 239075328 | bytes 644096 | tf_op jit(solution)/shard_map/while/body/eval_jaxpr/dot_general | solution.py:55
  203.1 6.7 %fusion.23 = f32[16,9,512]{2,1,0:T(8,128)S(1)} fusion(f32[16,9,512]{2,1,0:T(8,128)S(1)} %get-tuple-element.173, s32[]{:T(128)} %get-tuple-element.172, bf16[9,8192]{1,0:T(8,128)(2,1)S(1)} %get-tuple-element.190, bf16[16,8192]{1,0:T(8,128)(2,1)S(1)} %get-tuple-element.187, f32[8192]{0:T(1024)S(1)} %convert_element_type.44, f32[512]{0:T(512)S(1)} %bitcast.58, ...), kind=kOutput, calls=%fused_computation.3.clone.1 | convolution fusion | flops 239075328 | bytes 644096 | tf_op jit(solution)/shard_map/while/body/eval_jaxpr/dot_general | solution.py:55
  209.9 6.7 %fusion.23 = f32[16,9,512]{2,1,0:T(8,128)S(1)} fusion(f32[16,9,512]{2,1,0:T(8,128)S(1)} %get-tuple-element.173, s32[]{:T(128)} %get-tuple-element.172, bf16[9,8192]{1,0:T(8,128)(2,1)S(1)} %get-tuple-element.190, bf16[16,8192]{1,0:T(8,128)(2,1)S(1)} %get-tuple-element.187, f32[8192]{0:T(1024)S(1)} %convert_element_type.44, f32[512]{0:T(512)S(1)} %bitcast.58, ...), kind=kOutput, calls=%fused_computation.3.clone.1 | convolution fusion | flops 239075328 | bytes 644096 | tf_op jit(solution)/shard_map/while/body/eval_jaxpr/dot_general | solution.py:55
  216.7 6.7 %fusion.23 = f32[16,9,512]{2,1,0:T(8,128)S(1)} fusion(f32[16,9,512]{2,1,0:T(8,128)S(1)} %get-tuple-element.173, s32[]{:T(128)} %get-tuple-element.172, bf16[9,8192]{1,0:T(8,128)(2,1)S(1)} %get-tuple-element.190, bf16[16,8192]{1,0:T(8,128)(2,1)S(1)} %get-tuple-element.187, f32[8192]{0:T(1024)S(1)} %convert_element_type.44, f32[512]{0:T(512)S(1)} %bitcast.58, ...), kind=kOutput, calls=%fused_computation.3.clone.1 | convolution fusion | flops 239075328 | bytes 644096 | tf_op jit(solution)/shard_map/while/body/eval_jaxpr/dot_general | solution.py:55
  223.5 6.7 %fusion.23 = f32[16,9,512]{2,1,0:T(8,128)S(1)} fusion(f32[16,9,512]{2,1,0:T(8,128)S(1)} %get-tuple-element.173, s32[]{:T(128)} %get-tuple-element.172, bf16[9,8192]{1,0:T(8,128)(2,1)S(1)} %get-tuple-element.190, bf16[16,8192]{1,0:T(8,128)(2,1)S(1)} %get-tuple-element.187, f32[8192]{0:T(1024)S(1)} %convert_element_type.44, f32[512]{0:T(512)S(1)} %bitcast.58, ...), kind=kOutput, calls=%fused_computation.3.clone.1 | convolution fusion | flops 239075328 | bytes 644096 | tf_op jit(solution)/shard_map/while/body/eval_jaxpr/dot_general | solution.py:55
  230.2 6.7 %fusion.23 = f32[16,9,512]{2,1,0:T(8,128)S(1)} fusion(f32[16,9,512]{2,1,0:T(8,128)S(1)} %get-tuple-element.173, s32[]{:T(128)} %get-tuple-element.172, bf16[9,8192]{1,0:T(8,128)(2,1)S(1)} %get-tuple-element.190, bf16[16,8192]{1,0:T(8,128)(2,1)S(1)} %get-tuple-element.187, f32[8192]{0:T(1024)S(1)} %convert_element_type.44, f32[512]{0:T(512)S(1)} %bitcast.58, ...), kind=kOutput, calls=%fused_computation.3.clone.1 | convolution fusion | flops 239075328 | bytes 644096 | tf_op jit(solution)/shard_map/while/body/eval_jaxpr/dot_general | solution.py:55
  237.0 6.7 %fusion.23 = f32[16,9,512]{2,1,0:T(8,128)S(1)} fusion(f32[16,9,512]{2,1,0:T(8,128)S(1)} %get-tuple-element.173, s32[]{:T(128)} %get-tuple-element.172, bf16[9,8192]{1,0:T(8,128)(2,1)S(1)} %get-tuple-element.190, bf16[16,8192]{1,0:T(8,128)(2,1)S(1)} %get-tuple-element.187, f32[8192]{0:T(1024)S(1)} %convert_element_type.44, f32[512]{0:T(512)S(1)} %bitcast.58, ...), kind=kOutput, calls=%fused_computation.3.clone.1 | convolution fusion | flops 239075328 | bytes 644096 | tf_op jit(solution)/shard_map/while/body/eval_jaxpr/dot_general | solution.py:55
  243.8 6.7 %fusion.23 = f32[16,9,512]{2,1,0:T(8,128)S(1)} fusion(f32[16,9,512]{2,1,0:T(8,128)S(1)} %get-tuple-element.173, s32[]{:T(128)} %get-tuple-element.172, bf16[9,8192]{1,0:T(8,128)(2,1)S(1)} %get-tuple-element.190, bf16[16,8192]{1,0:T(8,128)(2,1)S(1)} %get-tuple-element.187, f32[8192]{0:T(1024)S(1)} %convert_element_type.44, f32[512]{0:T(512)S(1)} %bitcast.58, ...), kind=kOutput, calls=%fused_computation.3.clone.1 | convolution fusion | flops 239075328 | bytes 644096 | tf_op jit(solution)/shard_map/while/body/eval_jaxpr/dot_general | solution.py:55
  250.6 0.2 copy.19
  250.8 0.1 pad.1
  250.8 1.1 copy.26
  251.9 0.0 reduce-scatter.2.cloned.1.call-update
  252.0 51.0 %reduce-scatter.2.cloned.1.call-done = f32[9,512]{1,0:T(8,128)} async-done(((f32[9,8192]{1,0:T(8,128)}), f32[9,512]{1,0:T(8,128)}) %reduce-scatter.2.cloned.1.call-update) | async-done | bytes 18448 | tf_op jit(solution)/shard_map/reduce_scatter | solution.py:61
  302.9 0.7 slice.19
  303.6 0.7 slice_divide_fusion
  304.4 0.1 multiply_reduce_fusion.2
  304.4 0.1 copy.20
  304.5 85.7 %psum.7 = f32[8,8]{0,1:T(8,128)S(1)} all-reduce(f32[8,8]{0,1:T(8,128)S(1)} %copy.20), channel_id=1, replica_groups=mesh['row'=16,'col'=16] {'row','col'}, use_global_device_ids=true, to_apply=%region_6.7 | all-reduce | flops 64 | bytes 512 | tf_op jit(solution)/shard_map/psum | solution.py:64
  390.2 0.1 copy.21
  390.3 0.7 cholesky.16
  391.0 0.6 compare_reduce_fusion
  391.7 0.6 fusion.10
  392.3 0.6 custom-call.6
  393.0 0.8 convolution_multiply_fusion
  (56 shorter events, 0.5 us)
Async XLA Ops:
  6.5 64.4 %copy-start.1 = (bf16[512]{0:T(512)(128)(2,1)S(1)}, bf16[512]{0:T(512)(128)(2,1)}, u32[]{:S(2)}) copy-start(bf16[512]{0:T(512)(128)(2,1)} %param.6) | copy-start | bytes 3076
  6.5 296.4 %reduce-scatter.2.cloned.1.call-start = ((), (), s32[]{:S(2)}) async-start(), calls=%async_computation.1 | async-start | bytes 557056 | tf_op jit(solution)/shard_map/reduce_scatter | solution.py:61
  113.2 0.7 copy-start
Sparse Core Ops, SparseCore 0:
  252.1 50.7 reduce-scatter.1
where the time goes:
time: 401 us
  blocking collectives  220 us (55%)
  matrix products  109 us (27%)
  waiting for transfers between devices  51 us (13%)
  between operations  13.5 us (3%)
    dot_general x16, matrix products, one_block(): lax.dot_general(col_ext, affinity, (((1,), (1,)), ((), ())), preferred_el...  108 us
    psum x1, blocking collectives, shards(): gram = lax.psum(gram_local, ('row', 'col'))  85.7 us
    reduce_scatter x1, waiting for transfers between devices, shards(): total = lax.psum_scatter(row_part, 'col', scatter_dimension=1, tiled=True)  51 us
    all_gather x1, blocking collectives, shards(): lax.all_gather(points, 'row', axis=1, tiled=True)  32.8 us
    all_gather x1, blocking collectives, shards(): lax.all_gather(points, 'col', axis=1, tiled=True)  31.7 us
    all_gather x1, blocking collectives, shards(): lax.all_gather(vectors, 'row', axis=1, tiled=True)  27.9 us
    all_gather x1, blocking collectives, shards(): lax.all_gather(spread, 'col', axis=0, tiled=True)  22.7 us
    all_gather x1, blocking collectives, shards(): lax.all_gather(spread, 'row', axis=0, tiled=True)  19.3 us
  transfers between devices with their start and end apart: 1, of which 1 were waited for; matrix products, arithmetic and copies ran while one was open for 0% of the time, Pallas kernels for 0%

commit v1 on v0

v1 whole, which is shorter than its diff:
```python
import functools
import math

import jax
import jax.numpy as jnp
from jax import lax
from jax.experimental import pallas as pl
from jax.experimental.pallas import tpu as pltpu
from jax.sharding import PartitionSpec as P

F32, BF16 = jnp.float32, jnp.bfloat16
MESH = pl.DeviceIdType.MESH
LOG2E = 1.4426950408889634
DEPTH = 128
PAD = 16
PIECES_LEFT = (0, 0, 1, 1, 0, 2)
PIECES_RIGHT = (0, 1, 0, 1, 2, 0)


def split3(x):
    high = x.astype(BF16)
    rest = x - high.astype(F32)
    mid = rest.astype(BF16)
    low = (rest - mid.astype(F32)).astype(BF16)
    return high, mid, low


def factor(block, left):
    pts = block[:16].astype(F32)
    tail = block[16:].astype(F32)
    inv = 1.0 / tail[9:10]
    w = pts * inv
    norm = jnp.sum(pts * pts, axis=0, keepdims=True) * inv
    if left:
        w = w * (2.0 * LOG2E)
        terms = (norm * -LOG2E, inv * -LOG2E)
        order = PIECES_LEFT
    else:
        terms = (inv, norm)
        order = PIECES_RIGHT
    pieces = split3(w)
    rows = lax.broadcasted_iota(jnp.int32, pts.shape, 0)
    extra = jnp.zeros_like(pts)
    for t, term in enumerate(terms):
        cut = split3(term)
        for k, p in enumerate(order):
            extra = jnp.where(rows == 6 * t + k, cut[p].astype(F32), extra)
    return jnp.concatenate(
        [pieces[p] for p in order] + [extra.astype(BF16), jnp.zeros(pts.shape, BF16)], axis=0
    )


def kernel(n_row, n_col, pts_ref, spread_ref, vec_ref, out_ref, own, got_r, got_c, right, left, part_r, part_c,
           in_r, in_c, gram, gsend, sems):
    half_r, half_c = n_row // 2, n_col // 2
    r, c = lax.axis_index("row"), lax.axis_index("col")
    local = pts_ref.shape[1]

    def at_row(d):
        return (lax.rem(r + d + n_row, n_row), c)

    def at_col(d):
        return (r, lax.rem(c + d + n_col, n_col))

    barrier = pltpu.get_barrier_semaphore()
    for d in range(1, n_row):
        pl.semaphore_signal(barrier, inc=1, device_id=at_row(d), device_id_type=MESH)
    for d in range(1, n_col):
        pl.semaphore_signal(barrier, inc=1, device_id=at_col(d), device_id_type=MESH)

    own[:16, :] = pts_ref[...]
    rows8 = lax.broadcasted_iota(jnp.int32, (8, local), 0)
    tail = jnp.where(rows8 == 0, 1.0, jnp.where(rows8 == 1, spread_ref[...].astype(F32), 0.0))
    own[16:, :] = jnp.concatenate([vec_ref[...].astype(F32), tail], axis=0).astype(BF16)

    pl.semaphore_wait(barrier, n_row + n_col - 2)

    def copy(src, dst, name, slot, device):
        send, recv = sems[name]
        return pltpu.make_async_remote_copy(
            src_ref=src, dst_ref=dst.at[slot], send_sem=send.at[slot], recv_sem=recv.at[slot],
            device_id=device, device_id_type=MESH)

    gets_c = {d: copy(own, got_c, "gather_c", d, at_row(-d)) for d in range(1, half_r + 1)}
    gets_r = {d: copy(own, got_r, "gather_r", d, at_col(-d)) for d in range(1, n_col)}
    for d in range(1, n_col):
        gets_r[d].start()
        if d in gets_c:
            gets_c[d].start()
    for d in range(n_col, half_r + 1):
        gets_c[d].start()
    got_r[0] = own[...]
    got_c[0] = own[...]

    part_r[...] = jnp.zeros_like(part_r)
    part_c[...] = jnp.zeros_like(part_c)
    for d in gets_r:
        gets_r[d].wait_recv()
    for d in gets_c:
        gets_c[d].wait_recv()

    def make_right(d, _):
        right[d] = factor(got_r[d], False)
        return 0

    def make_left(d, _):
        left[d] = jnp.transpose(factor(got_c[d], True))
        return 0

    lax.fori_loop(0, n_col, make_right, 0)
    lax.fori_loop(0, half_r + 1, make_left, 0)

    def pair(dr, dc, both):
        expo = jnp.dot(left[dr], right[dc], preferred_element_type=F32)
        affinity = jnp.exp2(expo).astype(BF16)
        part_r[dc] += jnp.dot(got_c[dr, 16:, :], affinity, preferred_element_type=F32)
        if both:
            part_c[dr] += lax.dot_general(
                got_r[dc, 16:, :], affinity, (((1,), (1,)), ((), ())), preferred_element_type=F32)

    def both_pair(dr):
        def step(dc, _):
            pair(dr, dc, True)
            return 0
        return step

    puts_r = {d: copy(part_r.at[d], in_r, "reduce_r", d, at_col(d)) for d in range(1, n_col)}
    puts_c = {d: copy(part_c.at[d], in_c, "reduce_c", d, at_row(d)) for d in range(1, half_r + 1)}

    for dr in (0, half_r):
        pair(dr, 0, False)
        pair(dr, half_c, False)
        lax.fori_loop(1, half_c, both_pair(dr), 0, unroll=True)
        if dr:
            puts_c[dr].start()

    def middle(dr, _):
        lax.fori_loop(0, n_col, both_pair(dr), 0, unroll=True)
        copy(part_c.at[dr], in_c, "reduce_c", dr, at_row(dr)).start()
        return 0

    lax.fori_loop(1, half_r, middle, 0)
    for d in puts_r:
        puts_r[d].start()
    total = part_r[0] + part_c[0]
    for d in puts_c:
        puts_c[d].wait_recv()
        total += in_c[d]
    for d in puts_r:
        puts_r[d].wait_recv()
        total += in_r[d]
    update = total[:8] / total[8:9]
    mine = lax.dot_general(
        update, update, (((1,), (1,)), ((), ())), precision=lax.Precision.HIGHEST, preferred_element_type=F32)

    pending = []
    gsend[...] = jnp.zeros_like(gsend)
    for stage, (count, place) in enumerate(((n_col, at_col), (n_row, at_row))):
        gsend[stage, :, :8] = mine
        puts = [copy(gsend.at[stage], gram.at[stage], ("gram_c", "gram_r")[stage], d, place(d)) for d in range(1, count)]
        for p in puts:
            p.start()
        acc = gsend[stage]
        for d, p in enumerate(puts, 1):
            p.wait_recv()
            acc += gram[stage, d]
        mine = acc[:, :8]
        pending += puts

    g, u = mine, update
    rows_g = lax.broadcasted_iota(jnp.int32, g.shape, 0)
    rows_u = lax.broadcasted_iota(jnp.int32, u.shape, 0)
    for k in range(8):
        scale = 1.0 / jnp.sqrt(g[k : k + 1, k : k + 1])
        row_g, row_u = g[k : k + 1] * scale, u[k : k + 1] * scale
        col = g[:, k : k + 1] * scale
        u = jnp.where(rows_u == k, row_u, jnp.where(rows_u > k, u - col * row_u, u))
        g = jnp.where(rows_g > k, g - col * row_g, g)
    out_ref[...] = u * math.sqrt(local * n_row * n_col)

    for group in (gets_r, gets_c, puts_r, puts_c):
        for p in group.values():
            p.wait_send()
    for p in pending:
        p.wait_send()


def run(n_row, n_col, *refs):
    refs, flat = refs[:-12], refs[-12:]
    names = ("gather_r", "gather_c", "reduce_r", "reduce_c", "gram_c", "gram_r")
    sems = {name: (flat[2 * i], flat[2 * i + 1]) for i, name in enumerate(names)}
    kernel(n_row, n_col, *refs, sems)


def solution(mesh):
    n_row, n_col = mesh.shape["row"], mesh.shape["col"]
    half_r = n_row // 2

    def shards(points, spread, vectors):
        local = points.shape[1]
        vmem = pl.BlockSpec(memory_space=pltpu.VMEM)
        counts = (n_col, half_r + 1, n_col, half_r + 1, n_col, n_row)
        most = max(n_row, n_col)
        return pl.pallas_call(
            functools.partial(run, n_row, n_col),
            out_shape=jax.ShapeDtypeStruct((8, local), F32),
            in_specs=[vmem] * 3,
            out_specs=vmem,
            scratch_shapes=[
                pltpu.VMEM((32, local), BF16),
                pltpu.VMEM((n_col, 32, local), BF16),
                pltpu.VMEM((half_r + 1, 32, local), BF16),
                pltpu.VMEM((n_col, DEPTH, local), BF16),
                pltpu.VMEM((half_r + 1, local, DEPTH), BF16),
                pltpu.VMEM((n_col, PAD, local), F32),
                pltpu.VMEM((half_r + 1, PAD, local), F32),
                pltpu.VMEM((n_col, PAD, local), F32),
                pltpu.VMEM((half_r + 1, PAD, local), F32),
                pltpu.VMEM((2, most, 8, 128), F32),
                pltpu.VMEM((2, 8, 128), F32),
            ] + [pltpu.SemaphoreType.DMA((n,)) for n in counts for _ in range(2)],
            compiler_params=pltpu.CompilerParams(
                collective_id=0, has_side_effects=True, vmem_limit_bytes=48 << 20),
            name="subspace",
        )(points, spread.reshape(1, local), vectors)

    in_specs = (P(None, ("row", "col")), P(("row", "col")), P(None, ("row", "col")))
    return jax.shard_map(shards, mesh=mesh, in_specs=in_specs, out_specs=P(None, ("row", "col")), check_vma=False)
```

time: 401 us -> 113 us (0.28)
  blocking collectives: 220 us -> 0 us
  Pallas kernels: 0 us -> 110 us
  matrix products: 109 us -> 0 us
  waiting for transfers between devices: 51 us -> 0 us
  between operations: 13.5 us -> 0.01 us
    all_gather x5 -> x0, blocking collectives: 134 us -> none  [the longest x1 32.8 us: shards(): lax.all_gather(points, 'row', axis=1, tiled=True)]
    pallas_call x0 -> x1, Pallas kernels: none -> 110 us  [shards(): pl.pallas_call(functools.partial(run, n_row, n_col), out_shape=jax.ShapeD...]
    dot_general x16 -> x0, matrix products: 108 us -> none  [one_block(): lax.dot_general(col_ext, affinity, (((1,), (1,)), ((), ())), preferred_el...]
    psum x1 -> x0, blocking collectives: 85.7 us -> none  [shards(): gram = lax.psum(gram_local, ('row', 'col'))]
    reduce_scatter x1 -> x0, waiting for transfers between devices: 51 us -> none  [shards(): total = lax.psum_scatter(row_part, 'col', scatter_dimension=1, tiled=True)]
  transfers between devices with their start and end apart: 1 -> 0, of which waited for: 1 -> 0; matrix products, arithmetic and copies ran while one was open for 0% -> 0% of each run, Pallas kernels for 0% -> 0%
where the time goes in v1:
time: 113 us
  Pallas kernels  110 us (97%)
  local copies, waits for them, and re-layouts  2.7 us (2%)
    pallas_call x1, Pallas kernels, shards(): pl.pallas_call(functools.partial(run, n_row, n_col), out_shape=jax.ShapeD...  110 us

profile of v1, /device:TPU:1, one launch (start us, length us, event | category | flops | bytes accessed | tf_op | source)
XLA Modules:
  0.0 112.5 jit_solution(15602758687971024967)
XLA Ops:
  0.0 0.7 reshape.3.refs_1_
  0.7 0.0 copy-start
  0.7 0.7 copy-done
  1.4 0.0 copy-start.1
  1.4 0.7 copy-done.1
  2.1 109.8 %subspace.1 = f32[8,512]{1,0:T(8,128)S(1)} custom-call(bf16[16,512]{1,0:T(8,128)(2,1)S(1)} %copy-done, bf16[1,512]{1,0:T(2,128)(2,1)S(1)} %reshape.3.refs_1_, bf16[8,512]{1,0:T(8,128)(2,1)S(1)} %copy-done.1), custom_call_target="tpu_custom_call" | custom-call | tf_op jit(solution)/shard_map/subspace/pallas_call | solution.py:204
  111.9 0.6 copy.5
Async XLA Ops:
  0.7 0.7 copy-start
  1.4 0.7 copy-start.1

commit v2 on v1

v2 whole, which is shorter than its diff:
```python
import functools
import math

import jax
import jax.numpy as jnp
from jax import lax
from jax.experimental import pallas as pl
from jax.experimental.pallas import tpu as pltpu
from jax.sharding import PartitionSpec as P

F32, BF16 = jnp.float32, jnp.bfloat16
MESH = pl.DeviceIdType.MESH
LOG2E = 1.4426950408889634
DEPTH = 128
PAD = 16
PIECES_LEFT = (0, 0, 1, 1, 0, 2)
PIECES_RIGHT = (0, 1, 0, 1, 2, 0)


def split3(x):
    high = x.astype(BF16)
    rest = x - high.astype(F32)
    mid = rest.astype(BF16)
    low = (rest - mid.astype(F32)).astype(BF16)
    return high, mid, low


def factor(block, left):
    pts = block[:16].astype(F32)
    tail = block[16:].astype(F32)
    inv = 1.0 / tail[9:10]
    w = pts * inv
    norm = jnp.sum(pts * pts, axis=0, keepdims=True) * inv
    if left:
        w = w * (2.0 * LOG2E)
        terms = (norm * -LOG2E, inv * -LOG2E)
        order = PIECES_LEFT
    else:
        terms = (inv, norm)
        order = PIECES_RIGHT
    pieces = split3(w)
    rows = lax.broadcasted_iota(jnp.int32, pts.shape, 0)
    extra = jnp.zeros_like(pts)
    for t, term in enumerate(terms):
        cut = split3(term)
        for k, p in enumerate(order):
            extra = jnp.where(rows == 6 * t + k, cut[p].astype(F32), extra)
    return jnp.concatenate(
        [pieces[p] for p in order] + [extra.astype(BF16), jnp.zeros(pts.shape, BF16)], axis=0
    )


def kernel(n_row, n_col, pts_ref, spread_ref, vec_ref, out_ref, own, spread_v, vec_v, got_r, got_c, right, left,
           part_r, part_c, out_r, out_c, in_r, in_c, gram, gsend, aff, aff_t, load_sem, sems):
    half_r, half_c = n_row // 2, n_col // 2
    chunks = own.shape[1] // 128
    r, c = lax.axis_index("row"), lax.axis_index("col")
    local = own.shape[1]

    def at_row(d):
        return (lax.rem(r + d + n_row, n_row), c)

    def at_col(d):
        return (r, lax.rem(c + d + n_col, n_col))

    barrier = pltpu.get_barrier_semaphore()
    for d in range(1, n_col):
        pl.semaphore_signal(barrier, inc=1, device_id=at_col(d), device_id_type=MESH)
    for d in range(1, n_row):
        pl.semaphore_signal(barrier, inc=1, device_id=at_row(d), device_id_type=MESH)

    loads = [
        pltpu.make_async_copy(pts_ref, own.at[:16, :], load_sem.at[0]),
        pltpu.make_async_copy(vec_ref, vec_v, load_sem.at[1]),
        pltpu.make_async_copy(spread_ref, spread_v, load_sem.at[2]),
    ]
    for load in loads:
        load.start()
    part_r[...] = jnp.zeros_like(part_r)
    part_c[...] = jnp.zeros_like(part_c)
    gsend[...] = jnp.zeros_like(gsend)
    for load in loads:
        load.wait()
    rows8 = lax.broadcasted_iota(jnp.int32, (8, local), 0)
    spread = spread_v[...].astype(F32).reshape(1, local)
    tail = jnp.where(rows8 == 0, 1.0, jnp.where(rows8 == 1, spread, 0.0))
    own[16:, :] = jnp.concatenate([vec_v[...].astype(F32), tail], axis=0).astype(BF16)
    got_r[0] = own[...]
    got_c[0] = own[...]

    def copy(src, dst, name, slot, device):
        send, recv = sems[name]
        return pltpu.make_async_remote_copy(
            src_ref=src, dst_ref=dst.at[slot], send_sem=send.at[slot], recv_sem=recv.at[slot],
            device_id=device, device_id_type=MESH)

    def get_r(d):
        return copy(own, got_r, "gather_r", d, at_col(-d))

    def get_c(d):
        return copy(own, got_c, "gather_c", d, at_row(-d))

    def put_r(d):
        return copy(out_r.at[d], in_r, "reduce_r", d, at_col(d))

    def put_c(d):
        return copy(out_c.at[d], in_c, "reduce_c", d, at_row(d))

    def pack(dst, src):
        for n in range(chunks):
            lanes = pl.ds(128 * n, 128)
            dst[pl.ds(8 * n, 8), :] = src[:8, lanes]
            dst[pl.ds(8 * chunks + n, 1), :] = src[8:9, lanes]

    def add(totals, packed):
        product, degree = totals
        parts = [packed[pl.ds(8 * n, 8), :] for n in range(chunks)]
        degrees = packed[pl.ds(8 * chunks, chunks), :]
        return tuple(a + b for a, b in zip(product, parts)), degree + degrees

    def send_r(d):
        pack(out_r.at[d], part_r.at[d])
        put_r(d).start()

    def send_c(d):
        pack(out_c.at[d], part_c.at[d])
        put_c(d).start()

    def make_right(d):
        right[d] = factor(got_r[d], False)

    def make_left(d):
        left[d] = jnp.transpose(factor(got_c[d], True))

    def take_r(d):
        get_r(d).wait_recv()
        make_right(d)

    def take_c(d):
        get_c(d).wait_recv()
        make_left(d)

    def produce(slot, dr, dc, both=True):
        expo = jnp.dot(left[dr], right[dc], preferred_element_type=F32)
        affinity = jnp.exp2(expo).astype(BF16)
        aff[slot] = affinity
        if both:
            aff_t[slot] = jnp.transpose(affinity)

    def consume(slot, dr, dc, both=True):
        part_r[dc] += jnp.dot(got_c[dr, 16:, :], aff[slot], preferred_element_type=F32)
        if both:
            part_c[dr] += jnp.dot(got_r[dc, 16:, :], aff_t[slot], preferred_element_type=F32)

    make_right(0)
    make_left(0)
    produce(0, 0, 0, False)

    pl.semaphore_wait(barrier, n_row + n_col - 2)
    for d in range(1, half_c + 1):
        get_r(d).start()
    for d in range(1, half_r):
        get_c(d).start()
    for d in range(half_c + 1, n_col):
        get_r(d).start()
    get_c(half_r).start()

    for d in range(1, half_c + 1):
        take_r(d)
        produce(d % 2, 0, d, d < half_c)
        consume((d - 1) % 2, 0, d - 1, d > 1)
    take_c(1)
    produce((half_c + 1) % 2, 1, 0)
    consume(half_c % 2, 0, half_c, False)

    passes = half_r - 1

    def middle(t, _):
        far = t // passes
        dr = 1 + t - far * passes
        base = far * half_c
        after = t + 1
        far_after = after // passes
        last = after == 2 * passes
        dr_after = jnp.where(last, half_r, 1 + after - far_after * passes)
        base_after = jnp.where(last, half_c, far_after * half_c)

        @pl.when(t < passes - 1)
        def _():
            take_c(dr + 1)

        @pl.when(t == passes - 1)
        def _():
            for d in range(half_c + 1, n_col):
                take_r(d)
            take_c(half_r)

        @pl.when(t > passes + 1)
        def _():
            send_c(t - passes - 1)

        for k in range(half_c):
            slot = (half_c + 1 + k) % 2
            if k < half_c - 1:
                produce(1 - slot, dr, base + k + 1)
            else:
                produce(1 - slot, dr_after, base_after)
            consume(slot, dr, base + k)
        return 0

    lax.fori_loop(0, 2 * passes, middle, 0)
    for d in range(max(1, passes - 1), passes + 1):
        send_c(d)
    for d in range(half_c + 1, n_col):
        send_r(d)

    order = [half_c, 0] + list(range(1, half_c))
    for n, d in enumerate(order):
        slot = (half_c + 1 + n) % 2
        if n + 1 < len(order):
            produce(1 - slot, half_r, order[n + 1], n >= 1)
        consume(slot, half_r, d, n >= 2)
        if d:
            send_r(d)
    send_c(half_r)

    part_r[0] += part_c[0]
    pack(out_r.at[0], part_r.at[0])
    totals = (tuple(jnp.zeros((8, 128), F32) for _ in range(chunks)), jnp.zeros((chunks, 128), F32))
    totals = add(totals, out_r.at[0])
    for d in range(1, half_r):
        put_c(d).wait_recv()
        totals = add(totals, in_c.at[d])
    for d in list(range(half_c + 1, n_col)) + order:
        if d:
            put_r(d).wait_recv()
            totals = add(totals, in_r.at[d])
    put_c(half_r).wait_recv()
    product, degree = add(totals, in_c.at[half_r])
    update = jnp.concatenate([product[n] / degree[n : n + 1] for n in range(chunks)], axis=1)
    mine = lax.dot_general(
        update, update, (((1,), (1,)), ((), ())), precision=lax.Precision.HIGHEST, preferred_element_type=F32)

    pending = []
    for stage, (count, place) in enumerate(((n_col, at_col), (n_row, at_row))):
        gsend[stage, :, :8] = mine
        puts = [copy(gsend.at[stage], gram.at[stage], ("gram_c", "gram_r")[stage], d, place(d)) for d in range(1, count)]
        for p in puts:
            p.start()
        acc = gsend[stage]
        for d, p in enumerate(puts, 1):
            p.wait_recv()
            acc += gram[stage, d]
        mine = acc[:, :8]
        pending += puts

    g, u = mine, update
    rows_g = lax.broadcasted_iota(jnp.int32, g.shape, 0)
    rows_u = lax.broadcasted_iota(jnp.int32, u.shape, 0)
    for k in range(8):
        scale = 1.0 / jnp.sqrt(g[k : k + 1, k : k + 1])
        row_g, row_u = g[k : k + 1] * scale, u[k : k + 1] * scale
        col = g[:, k : k + 1] * scale
        u = jnp.where(rows_u == k, row_u, jnp.where(rows_u > k, u - col * row_u, u))
        g = jnp.where(rows_g > k, g - col * row_g, g)
    out_ref[...] = u * math.sqrt(local * n_row * n_col)

    for d in range(1, n_col):
        get_r(d).wait_send()
        put_r(d).wait_send()
    for d in range(1, half_r + 1):
        get_c(d).wait_send()
        put_c(d).wait_send()
    for p in pending:
        p.wait_send()


def run(n_row, n_col, *refs):
    refs, flat = refs[:-12], refs[-12:]
    names = ("gather_r", "gather_c", "reduce_r", "reduce_c", "gram_c", "gram_r")
    sems = {name: (flat[2 * i], flat[2 * i + 1]) for i, name in enumerate(names)}
    kernel(n_row, n_col, *refs, sems)


def solution(mesh):
    n_row, n_col = mesh.shape["row"], mesh.shape["col"]
    half_r = n_row // 2

    def shards(points, spread, vectors):
        local = points.shape[1]
        vmem = pl.BlockSpec(memory_space=pltpu.VMEM)
        counts = (n_col, half_r + 1, n_col, half_r + 1, n_col, n_row)
        most = max(n_row, n_col)
        packed = -(-9 * (local // 128) // 8) * 8
        return pl.pallas_call(
            functools.partial(run, n_row, n_col),
            out_shape=jax.ShapeDtypeStruct((8, local), F32),
            in_specs=[pl.BlockSpec(memory_space=pl.ANY)] * 3,
            out_specs=vmem,
            scratch_shapes=[
                pltpu.VMEM((32, local), BF16),
                pltpu.VMEM((local,), BF16),
                pltpu.VMEM((8, local), BF16),
                pltpu.VMEM((n_col, 32, local), BF16),
                pltpu.VMEM((half_r + 1, 32, local), BF16),
                pltpu.VMEM((n_col, DEPTH, local), BF16),
                pltpu.VMEM((half_r + 1, local, DEPTH), BF16),
                pltpu.VMEM((n_col, PAD, local), F32),
                pltpu.VMEM((half_r + 1, PAD, local), F32),
                pltpu.VMEM((n_col, packed, 128), F32),
                pltpu.VMEM((half_r + 1, packed, 128), F32),
                pltpu.VMEM((n_col, packed, 128), F32),
                pltpu.VMEM((half_r + 1, packed, 128), F32),
                pltpu.VMEM((2, most, 8, 128), F32),
                pltpu.VMEM((2, 8, 128), F32),
                pltpu.VMEM((2, local, local), BF16),
                pltpu.VMEM((2, local, local), BF16),
                pltpu.SemaphoreType.DMA((3,)),
            ] + [pltpu.SemaphoreType.DMA((n,)) for n in counts for _ in range(2)],
            compiler_params=pltpu.CompilerParams(
                collective_id=0, has_side_effects=True, vmem_limit_bytes=48 << 20),
            name="subspace",
        )(points, spread, vectors)

    in_specs = (P(None, ("row", "col")), P(("row", "col")), P(None, ("row", "col")))
    return jax.shard_map(shards, mesh=mesh, in_specs=in_specs, out_specs=P(None, ("row", "col")), check_vma=False)
```

time: 113 us -> 83.7 us (0.74)
  Pallas kernels: 110 us -> 80.8 us
    pallas_call x1, Pallas kernels: 110 us -> 80.8 us  [shards(): pl.pallas_call(functools.partial(run, n_row, n_col), out_shape=jax.ShapeD...]
    unnamed x5 -> x7, local copies, waits for them, and re-layouts: 2.02 us -> 2.7 us
where the time goes in v2:
time: 83.7 us; the launch traced here: 83.5 us
  Pallas kernels  80.8 us (97%)
  local copies, waits for them, and re-layouts  2.7 us (3%)
    pallas_call x1, Pallas kernels, shards(): pl.pallas_call(functools.partial(run, n_row, n_col), out_shape=jax.ShapeD...  80.8 us
    unnamed x7, local copies, waits for them, and re-layouts  2.7 us

profile of v2, /device:TPU:1, one launch (start us, length us, event | category | flops | bytes accessed | tf_op | source)
XLA Modules:
  0.0 83.5 jit_solution(4745134664352451419)
XLA Ops:
  0.0 0.0 copy-start
  0.0 0.7 copy-done
  0.7 0.0 copy-start.1
  0.7 0.7 copy-done.1
  1.4 0.0 copy-start.2
  1.4 0.7 copy-done.2
  2.1 80.8 %subspace.1 = f32[8,512]{1,0:T(8,128)S(1)} custom-call(bf16[16,512]{1,0:T(8,128)(2,1)S(1)} %copy-done, bf16[512]{0:T(512)(128)(2,1)S(1)} %copy-done.2, bf16[8,512]{1,0:T(8,128)(2,1)S(1)} %copy-done.1), custom_call_target="tpu_custom_call" | custom-call | tf_op jit(solution)/shard_map/subspace/pallas_call | solution.py:295
  82.9 0.6 copy.5
Async XLA Ops:
  0.0 0.7 copy-start
  0.7 0.7 copy-start.1
  1.4 0.7 copy-start.2

commit v3 on v2

--- a/solution.py
+++ b/solution.py
@@ -140,103 +140,140 @@
         get_c(d).wait_recv()
         make_left(d)
 
-    def produce(slot, dr, dc, both=True):
-        expo = jnp.dot(left[dr], right[dc], preferred_element_type=F32)
+    half = local // 2
+
+    def produce_part(slot, dr, dc, both, rows, lanes):
+        expo = jnp.dot(left[dr, rows, :], right[dc, :, lanes], preferred_element_type=F32)
         affinity = jnp.exp2(expo).astype(BF16)
-        aff[slot] = affinity
+        aff[slot, rows, lanes] = affinity
         if both:
-            aff_t[slot] = jnp.transpose(affinity)
-
-    def consume(slot, dr, dc, both=True):
-        part_r[dc] += jnp.dot(got_c[dr, 16:, :], aff[slot], preferred_element_type=F32)
-        if both:
-            part_c[dr] += jnp.dot(got_r[dc, 16:, :], aff_t[slot], preferred_element_type=F32)
+            aff_t[slot, lanes, rows] = jnp.transpose(affinity)
+
+    def use_columns(slot, dr, dc, lanes):
+        part_r[dc, :, lanes] += jnp.dot(got_c[dr, 16:, :], aff[slot, :, lanes], preferred_element_type=F32)
+
+    def use_rows(slot, dr, dc, rows):
+        part_c[dr, :, rows] += jnp.dot(got_r[dc, 16:, :], aff_t[slot, :, rows], preferred_element_type=F32)
+
+    def step(cur, after):
+        for q in range(4):
+            rows, lanes = pl.ds((q // 2) * half, half), pl.ds((q % 2) * half, half)
+            if after is not None:
+                produce_part(*after, rows, lanes)
+            if cur is not None:
+                slot, dr, dc, both = cur
+                part = pl.ds((q % 2) * half, half)
+                if q < 2:
+                    use_columns(slot, dr, dc, part)
+                elif both:
+                    use_rows(slot, dr, dc, part)
 
     make_right(0)
     make_left(0)
-    produce(0, 0, 0, False)
+    step(None, (0, 0, 0, False))
 
     pl.semaphore_wait(barrier, n_row + n_col - 2)
     for d in range(1, half_c + 1):
         get_r(d).start()
-    for d in range(1, half_r):
+    get_c(1).start()
+    far_r = range(half_c + 1, n_col)
+
+    for d in range(1, half_c + 1):
+        if 1 < d < half_r:
+            get_c(d).start()
+        take_r(d)
+        step(((d - 1) % 2, 0, d - 1, d > 1), (d % 2, 0, d, d < half_c))
+    for d in range(half_c + 1, half_r):
         get_c(d).start()
-    for d in range(half_c + 1, n_col):
-        get_r(d).start()
-    get_c(half_r).start()
-
-    for d in range(1, half_c + 1):
-        take_r(d)
-        produce(d % 2, 0, d, d < half_c)
-        consume((d - 1) % 2, 0, d - 1, d > 1)
+    done = half_c + 1
     take_c(1)
-    produce((half_c + 1) % 2, 1, 0)
-    consume(half_c % 2, 0, half_c, False)
-
-    passes = half_r - 1
-
-    def middle(t, _):
-        far = t // passes
-        dr = 1 + t - far * passes
-        base = far * half_c
-        after = t + 1
-        far_after = after // passes
-        last = after == 2 * passes
-        dr_after = jnp.where(last, half_r, 1 + after - far_after * passes)
-        base_after = jnp.where(last, half_c, far_after * half_c)
-
-        @pl.when(t < passes - 1)
+    step((1 - done % 2, 0, half_c, False), (done % 2, 1, 0, True))
+
+    def near(t, _):
+        dr = t + 1
+
+        @pl.when(t == 0)
+        def _():
+            for d in far_r:
+                get_r(d).start()
+            get_c(half_r).start()
+
+        @pl.when(t < half_r - 2)
         def _():
             take_c(dr + 1)
 
-        @pl.when(t == passes - 1)
+        @pl.when(t == half_r - 2)
         def _():
-            for d in range(half_c + 1, n_col):
-                take_r(d)
             take_c(half_r)
 
-        @pl.when(t > passes + 1)
-        def _():
-            send_c(t - passes - 1)
-
+        wrap = t == half_r - 2
+        dr_after = dr + 1
+        dc_after = jnp.where(wrap, half_c, 0)
         for k in range(half_c):
-            slot = (half_c + 1 + k) % 2
-            if k < half_c - 1:
-                produce(1 - slot, dr, base + k + 1)
-            else:
-                produce(1 - slot, dr_after, base_after)
-            consume(slot, dr, base + k)
+            slot = (done + k) % 2
+            after = (dr, k + 1) if k < half_c - 1 else (dr_after, dc_after)
+            step((slot, dr, k, True), (1 - slot, *after, True))
         return 0
 
-    lax.fori_loop(0, 2 * passes, middle, 0)
-    for d in range(max(1, passes - 1), passes + 1):
-        send_c(d)
-    for d in range(half_c + 1, n_col):
-        send_r(d)
-
+    lax.fori_loop(0, half_r - 1, near, 0)
+    done += (half_r - 1) * half_c
+
+    for d in far_r:
+        take_r(d)
     order = [half_c, 0] + list(range(1, half_c))
     for n, d in enumerate(order):
-        slot = (half_c + 1 + n) % 2
-        if n + 1 < len(order):
-            produce(1 - slot, half_r, order[n + 1], n >= 1)
-        consume(slot, half_r, d, n >= 2)
-        if d:
-            send_r(d)
+        slot = (done + n) % 2
+        after = (half_r, order[n + 1], n >= 1) if n + 1 < len(order) else (1, half_c, True)
+        step((slot, half_r, d, n >= 2), (1 - slot, *after))
+    done += len(order)
     send_c(half_r)
+    for d in range(1, half_c):
+        send_r(d)
+
+    def far(t, last):
+        dc = half_c + 2 * t
+        pairs = [(dc + e, dr) for e in range(2) for dr in range(1, half_r)]
+        if not last:
+            @pl.when(t > 0)
+            def _():
+                send_r(dc - 2)
+                send_r(dc - 1)
+        elif half_c > 2:
+            send_r(dc - 2)
+            send_r(dc - 1)
+        for n, (d, dr) in enumerate(pairs):
+            slot = (done + n) % 2
+            after = None
+            if n + 1 < len(pairs):
+                after = (1 - slot, pairs[n + 1][1], pairs[n + 1][0], True)
+            elif not last:
+                after = (1 - slot, 1, dc + 2, True)
+            step((slot, dr, d, True), after)
+            if last and n == half_r - 2:
+                send_r(d)
+            if last and n >= half_r - 1:
+                send_c(dr)
+        if last:
+            send_r(dc + 1)
+        return 0
+
+    lax.fori_loop(0, half_c // 2 - 1, lambda t, _: far(t, False), 0)
+    far(half_c // 2 - 1, True)
 
     part_r[0] += part_c[0]
     pack(out_r.at[0], part_r.at[0])
     totals = (tuple(jnp.zeros((8, 128), F32) for _ in range(chunks)), jnp.zeros((chunks, 128), F32))
     totals = add(totals, out_r.at[0])
+    put_c(half_r).wait_recv()
+    totals = add(totals, in_c.at[half_r])
+    for d in range(1, n_col - 1):
+        put_r(d).wait_recv()
+        totals = add(totals, in_r.at[d])
     for d in range(1, half_r):
         put_c(d).wait_recv()
         totals = add(totals, in_c.at[d])
-    for d in list(range(half_c + 1, n_col)) + order:
-        if d:
-            put_r(d).wait_recv()
-            totals = add(totals, in_r.at[d])
-    put_c(half_r).wait_recv()
-    product, degree = add(totals, in_c.at[half_r])
+    put_r(n_col - 1).wait_recv()
+    product, degree = add(totals, in_r.at[n_col - 1])
     update = jnp.concatenate([product[n] / degree[n : n + 1] for n in range(chunks)], axis=1)
     mine = lax.dot_general(
         update, update, (((1,), (1,)), ((), ())), precision=lax.Precision.HIGHEST, preferred_element_type=F32)
@@ -244,12 +281,13 @@
     pending = []
     for stage, (count, place) in enumerate(((n_col, at_col), (n_row, at_row))):
         gsend[stage, :, :8] = mine
-        puts = [copy(gsend.at[stage], gram.at[stage], ("gram_c", "gram_r")[stage], d, place(d)) for d in range(1, count)]
+        puts = [copy(gsend.at[stage], gram.at[stage], ("gram_c", "gram_r")[stage], d, place(d)) for d in sorted(range(1, count), key=lambda d: -min(d % 8, 8 - d % 8))]
         for p in puts:
             p.start()
         acc = gsend[stage]
-        for d, p in enumerate(puts, 1):
+        for p in puts:
             p.wait_recv()
+        for d in range(1, count):
             acc += gram[stage, d]
         mine = acc[:, :8]
         pending += puts

time: 83.7 us -> 79.8 us (0.953)
  Pallas kernels: 80.8 us -> 76.8 us
    pallas_call x1, Pallas kernels: 80.8 us -> 76.8 us  [shards(): pl.pallas_call(functools.partial(run, n_row, n_col), out_shape=jax.ShapeD...]
where the time goes in v3:
time: 79.8 us; the launch traced here: 79.6 us
  Pallas kernels  76.8 us (96%)
  local copies, waits for them, and re-layouts  2.7 us (3%)
    pallas_call x1, Pallas kernels, shards(): pl.pallas_call(functools.partial(run, n_row, n_col), out_shape=jax.ShapeD...  76.8 us
    unnamed x7, local copies, waits for them, and re-layouts  2.7 us

profile of v3, /device:TPU:1, one launch (start us, length us, event | category | flops | bytes accessed | tf_op | source)
XLA Modules:
  0.0 79.6 jit_solution(18241248341130708477)
XLA Ops:
  0.0 0.0 copy-start
  0.0 0.7 copy-done
  0.7 0.0 copy-start.1
  0.7 0.7 copy-done.1
  1.4 0.0 copy-start.2
  1.4 0.7 copy-done.2
  2.1 76.8 %subspace.1 = f32[8,512]{1,0:T(8,128)S(1)} custom-call(bf16[16,512]{1,0:T(8,128)(2,1)S(1)} %copy-done, bf16[512]{0:T(512)(128)(2,1)S(1)} %copy-done.2, bf16[8,512]{1,0:T(8,128)(2,1)S(1)} %copy-done.1), custom_call_target="tpu_custom_call" | custom-call | tf_op jit(solution)/shard_map/subspace/pallas_call | solution.py:333
  78.9 0.6 copy.5
Async XLA Ops:
  0.0 0.7 copy-start
  0.7 0.7 copy-start.1
  1.4 0.7 copy-start.2

commit v4 on v3

--- a/solution.py
+++ b/solution.py
@@ -158,8 +158,6 @@
     def step(cur, after):
         for q in range(4):
             rows, lanes = pl.ds((q // 2) * half, half), pl.ds((q % 2) * half, half)
-            if after is not None:
-                produce_part(*after, rows, lanes)
             if cur is not None:
                 slot, dr, dc, both = cur
                 part = pl.ds((q % 2) * half, half)
@@ -167,56 +165,63 @@
                     use_columns(slot, dr, dc, part)
                 elif both:
                     use_rows(slot, dr, dc, part)
+            if after is not None:
+                produce_part(*after, rows, lanes)
 
     make_right(0)
     make_left(0)
     step(None, (0, 0, 0, False))
 
     pl.semaphore_wait(barrier, n_row + n_col - 2)
-    for d in range(1, half_c + 1):
-        get_r(d).start()
-    get_c(1).start()
     far_r = range(half_c + 1, n_col)
-
-    for d in range(1, half_c + 1):
-        if 1 < d < half_r:
-            get_c(d).start()
-        take_r(d)
-        step(((d - 1) % 2, 0, d - 1, d > 1), (d % 2, 0, d, d < half_c))
-    for d in range(half_c + 1, half_r):
-        get_c(d).start()
-    done = half_c + 1
-    take_c(1)
-    step((1 - done % 2, 0, half_c, False), (done % 2, 1, 0, True))
-
-    def near(t, _):
-        dr = t + 1
-
-        @pl.when(t == 0)
-        def _():
+    square = min(4, half_r, half_c)
+    for k in range(1, square):
+        get_r(k).start()
+        get_c(k).start()
+
+    head = [(0, 0, False)]
+    for k in range(1, square):
+        for d in range(k):
+            head += [(d, k, True), (k, d, True)]
+        head.append((k, k, True))
+    head += [(0, d, d < half_c) for d in range(square, half_c + 1)]
+    first_row = len(head)
+    head += [(dr, dc, True) for dr in range(1, square) for dc in range(square, half_c)]
+    following = (square, 0, True) if square < half_r else (half_r, half_c, False)
+    have_r, have_c = {0}, {0}
+    for n, pair in enumerate(head):
+        dr, dc, both = head[n + 1] if n + 1 < len(head) else following
+        if n + 1 == first_row:
             for d in far_r:
                 get_r(d).start()
             get_c(half_r).start()
-
-        @pl.when(t < half_r - 2)
-        def _():
-            take_c(dr + 1)
-
-        @pl.when(t == half_r - 2)
-        def _():
-            take_c(half_r)
-
-        wrap = t == half_r - 2
-        dr_after = dr + 1
-        dc_after = jnp.where(wrap, half_c, 0)
+        if dc not in have_r:
+            if dc == min(2, square):
+                for d in range(square, half_c + 1):
+                    get_r(d).start()
+            if dc == min(3, square):
+                for d in range(square, half_r):
+                    get_c(d).start()
+            take_r(dc)
+            have_r.add(dc)
+        if dr not in have_c:
+            take_c(dr)
+            have_c.add(dr)
+        step((n % 2, *pair), ((n + 1) % 2, dr, dc, both))
+    done = len(head)
+
+    def near(t, _):
+        dr = square + t
+        take_c(dr + 1)
+        wrap = dr == half_r - 1
         for k in range(half_c):
             slot = (done + k) % 2
-            after = (dr, k + 1) if k < half_c - 1 else (dr_after, dc_after)
+            after = (dr, k + 1) if k < half_c - 1 else (dr + 1, jnp.where(wrap, half_c, 0))
             step((slot, dr, k, True), (1 - slot, *after, True))
         return 0
 
-    lax.fori_loop(0, half_r - 1, near, 0)
-    done += (half_r - 1) * half_c
+    lax.fori_loop(0, half_r - square, near, 0)
+    done += (half_r - square) * half_c
 
     for d in far_r:
         take_r(d)
@@ -296,7 +301,7 @@
     rows_g = lax.broadcasted_iota(jnp.int32, g.shape, 0)
     rows_u = lax.broadcasted_iota(jnp.int32, u.shape, 0)
     for k in range(8):
-        scale = 1.0 / jnp.sqrt(g[k : k + 1, k : k + 1])
+        scale = lax.rsqrt(g[k : k + 1, k : k + 1])
         row_g, row_u = g[k : k + 1] * scale, u[k : k + 1] * scale
         col = g[:, k : k + 1] * scale
         u = jnp.where(rows_u == k, row_u, jnp.where(rows_u > k, u - col * row_u, u))

time: 79.8 us -> 78.8 us (0.987)
  Pallas kernels: 76.8 us -> 75.8 us
    pallas_call x1, Pallas kernels: 76.8 us -> 75.8 us  [shards(): pl.pallas_call(functools.partial(run, n_row, n_col), out_shape=jax.ShapeD...]
where the time goes in v4:
time: 78.8 us; the launch traced here: 78.5 us
  Pallas kernels  75.8 us (96%)
  local copies, waits for them, and re-layouts  2.7 us (3%)
    pallas_call x1, Pallas kernels, shards(): pl.pallas_call(functools.partial(run, n_row, n_col), out_shape=jax.ShapeD...  75.8 us
    unnamed x7, local copies, waits for them, and re-layouts  2.7 us

profile of v4, /device:TPU:1, one launch (start us, length us, event | category | flops | bytes accessed | tf_op | source)
XLA Modules:
  0.0 78.5 jit_solution(7904681255313169718)
XLA Ops:
  0.0 0.0 copy-start
  0.0 0.7 copy-done
  0.7 0.0 copy-start.1
  0.7 0.7 copy-done.1
  1.4 0.0 copy-start.2
  1.4 0.7 copy-done.2
  2.1 75.8 %subspace.1 = f32[8,512]{1,0:T(8,128)S(1)} custom-call(bf16[16,512]{1,0:T(8,128)(2,1)S(1)} %copy-done, bf16[512]{0:T(512)(128)(2,1)S(1)} %copy-done.2, bf16[8,512]{1,0:T(8,128)(2,1)S(1)} %copy-done.1), custom_call_target="tpu_custom_call" | custom-call | tf_op jit(solution)/shard_map/subspace/pallas_call | solution.py:338
  77.9 0.6 copy.5
Async XLA Ops:
  0.0 0.7 copy-start
  0.7 0.7 copy-start.1
  1.4 0.7 copy-start.2

commit v5 on v4

--- a/solution.py
+++ b/solution.py
@@ -157,7 +157,7 @@
 
     def step(cur, after):
         for q in range(4):
-            rows, lanes = pl.ds((q // 2) * half, half), pl.ds((q % 2) * half, half)
+            rows, lanes = pl.ds((q % 2) * half, half), pl.ds((q // 2) * half, half)
             if cur is not None:
                 slot, dr, dc, both = cur
                 part = pl.ds((q % 2) * half, half)
@@ -174,10 +174,12 @@
 
     pl.semaphore_wait(barrier, n_row + n_col - 2)
     far_r = range(half_c + 1, n_col)
-    square = min(4, half_r, half_c)
+    square = min(2, half_r, half_c)
     for k in range(1, square):
         get_r(k).start()
         get_c(k).start()
+    for d in range(square, half_c + 1):
+        get_r(d).start()
 
     head = [(0, 0, False)]
     for k in range(1, square):
@@ -196,10 +198,7 @@
                 get_r(d).start()
             get_c(half_r).start()
         if dc not in have_r:
-            if dc == min(2, square):
-                for d in range(square, half_c + 1):
-                    get_r(d).start()
-            if dc == min(3, square):
+            if dc == square:
                 for d in range(square, half_r):
                     get_c(d).start()
             take_r(dc)

time: 78.8 us -> 77.1 us (0.978)
  Pallas kernels: 75.8 us -> 74.1 us
    pallas_call x1, Pallas kernels: 75.8 us -> 74.1 us  [shards(): pl.pallas_call(functools.partial(run, n_row, n_col), out_shape=jax.ShapeD...]
where the time goes in v5:
time: 77.1 us; the launch traced here: 76.8 us
  Pallas kernels  74.1 us (96%)
  local copies, waits for them, and re-layouts  2.7 us (4%)
    pallas_call x1, Pallas kernels, shards(): pl.pallas_call(functools.partial(run, n_row, n_col), out_shape=jax.ShapeD...  74.1 us
    unnamed x7, local copies, waits for them, and re-layouts  2.7 us

profile of v5, /device:TPU:1, one launch (start us, length us, event | category | flops | bytes accessed | tf_op | source)
XLA Modules:
  0.0 76.8 jit_solution(17359690224373320029)
XLA Ops:
  0.0 0.0 copy-start
  0.0 0.7 copy-done
  0.7 0.0 copy-start.1
  0.7 0.7 copy-done.1
  1.4 0.0 copy-start.2
  1.4 0.7 copy-done.2
  2.1 74.1 %subspace.1 = f32[8,512]{1,0:T(8,128)S(1)} custom-call(bf16[16,512]{1,0:T(8,128)(2,1)S(1)} %copy-done, bf16[512]{0:T(512)(128)(2,1)S(1)} %copy-done.2, bf16[8,512]{1,0:T(8,128)(2,1)S(1)} %copy-done.1), custom_call_target="tpu_custom_call" | custom-call | tf_op jit(solution)/shard_map/subspace/pallas_call | solution.py:337
  76.2 0.6 copy.5
Async XLA Ops:
  0.0 0.7 copy-start
  0.7 0.7 copy-start.1
  1.4 0.7 copy-start.2

commit v6 on v5

--- a/solution.py
+++ b/solution.py
@@ -178,7 +178,8 @@
     for k in range(1, square):
         get_r(k).start()
         get_c(k).start()
-    for d in range(square, half_c + 1):
+    nearest = sorted(range(square, half_c + 1), key=lambda d: min(d % half_c, half_c - d % half_c))
+    for d in nearest:
         get_r(d).start()
 
     head = [(0, 0, False)]
@@ -186,19 +187,20 @@
         for d in range(k):
             head += [(d, k, True), (k, d, True)]
         head.append((k, k, True))
-    head += [(0, d, d < half_c) for d in range(square, half_c + 1)]
-    first_row = len(head)
-    head += [(dr, dc, True) for dr in range(1, square) for dc in range(square, half_c)]
+    for d in nearest:
+        head.append((0, d, d < half_c))
+        if d < half_c:
+            head += [(dr, d, True) for dr in range(1, square)]
     following = (square, 0, True) if square < half_r else (half_r, half_c, False)
     have_r, have_c = {0}, {0}
     for n, pair in enumerate(head):
         dr, dc, both = head[n + 1] if n + 1 < len(head) else following
-        if n + 1 == first_row:
+        if n + 2 == len(head):
             for d in far_r:
                 get_r(d).start()
             get_c(half_r).start()
         if dc not in have_r:
-            if dc == square:
+            if dc == nearest[0]:
                 for d in range(square, half_r):
                     get_c(d).start()
             take_r(dc)

time: 77.1 us -> 75.6 us (0.981)
  Pallas kernels: 74.1 us -> 72.6 us
    pallas_call x1, Pallas kernels: 74.1 us -> 72.6 us  [shards(): pl.pallas_call(functools.partial(run, n_row, n_col), out_shape=jax.ShapeD...]
where the time goes in v6:
time: 75.6 us; the launch traced here: 75.3 us
  Pallas kernels  72.6 us (96%)
  local copies, waits for them, and re-layouts  2.7 us (4%)
    pallas_call x1, Pallas kernels, shards(): pl.pallas_call(functools.partial(run, n_row, n_col), out_shape=jax.ShapeD...  72.6 us
    unnamed x7, local copies, waits for them, and re-layouts  2.7 us

profile of v6, /device:TPU:1, one launch (start us, length us, event | category | flops | bytes accessed | tf_op | source)
XLA Modules:
  0.0 75.3 jit_solution(548393234065571434)
XLA Ops:
  0.0 0.0 copy-start
  0.0 0.7 copy-done
  0.7 0.0 copy-start.1
  0.7 0.7 copy-done.1
  1.4 0.0 copy-start.2
  1.4 0.7 copy-done.2
  2.1 72.6 %subspace.1 = f32[8,512]{1,0:T(8,128)S(1)} custom-call(bf16[16,512]{1,0:T(8,128)(2,1)S(1)} %copy-done, bf16[512]{0:T(512)(128)(2,1)S(1)} %copy-done.2, bf16[8,512]{1,0:T(8,128)(2,1)S(1)} %copy-done.1), custom_call_target="tpu_custom_call" | custom-call | tf_op jit(solution)/shard_map/subspace/pallas_call | solution.py:339
  74.7 0.6 copy.5
Async XLA Ops:
  0.0 0.7 copy-start
  0.7 0.7 copy-start.1
  1.4 0.7 copy-start.2
